TPU v7x, 512 devices: a whole 4x8x8 slice. The times are simulated.
512 devices in a mesh: grp: 16 (over y, core), path: 32 (over z, x).
Axes of the slice: x: 4, y: 8, z: 8, core: 2. Of those that a mesh axis runs over, the one named last changes fastest.
Arguments:
- link_state: bfloat16 [16, 16384, 256], P('grp', 'path'), may hold values from -6 to 6
- path_state: bfloat16 [16, 4096, 256], P('grp', 'path'), may hold values from -6 to 6
- path_links: int32 [4096, 8], P('path'), may hold values from -1 to 16383, as said below
- w_path_in: bfloat16 [256, 768], replicated, may hold values from -0.375 to 0.375
- w_path_hid: bfloat16 [256, 768], replicated, may hold values from -0.375 to 0.375
- w_link_in: bfloat16 [256, 768], replicated, may hold values from -0.375 to 0.375
- w_link_hid: bfloat16 [256, 768], replicated, may hold values from -0.375 to 0.375
- cotangent: bfloat16 [16, 4096, 128], P('grp', 'path'), may hold values from -0.0234375 to 0.0234375
Outputs:
- link_next: bfloat16 [16, 16384, 256], P('grp', 'path')
- path_final: bfloat16 [16, 4096, 256], P('grp', 'path')
- read_grad: float32 [128, 256], P('path')
Inputs may be any that keep to these rules, and one draw needn't show every extreme that they name: `path_links`: entry -1 marks no hop; each path's live entries come first and number two or more. In the rows of one device, at most 32 live entries name links of the block of 512 link ids held by any one index of path, and some block takes exactly 32.
All inputs are finite; a program needn't handle non-finite values.
Results may differ from a plain program's by a relative error of at most 0.0035.
Values may be sent and summed in bfloat16 or wider, within the bound.
A program may use at most 64 MiB of HBM per device.

v0:
```python
import jax
import jax.numpy as jnp
from jax import lax
from jax.sharding import PartitionSpec as P


def gated_update(projected, carried, w_hidden):
    width = carried.shape[1]
    recur = jnp.dot(carried.astype(jnp.bfloat16), w_hidden, preferred_element_type=jnp.float32)
    reset = jax.nn.sigmoid(projected[:, :width] + recur[:, :width])
    update = jax.nn.sigmoid(projected[:, width : 2 * width] + recur[:, width : 2 * width])
    candidate = jnp.tanh(projected[:, 2 * width :] + reset * recur[:, 2 * width :])
    return (1.0 - update) * candidate + update * carried


def shards(
    link_state, path_state, path_links, w_path_in, w_path_hid, w_link_in, w_link_hid, cotangent
):
    own_links = link_state[0]
    link_dev, width = own_links.shape
    peer_count = lax.axis_size("path")
    path_count, hop_count = path_links.shape
    flat_ids = path_links.reshape(-1)
    is_live = flat_ids >= 0
    owner_id = jnp.where(is_live, flat_ids // link_dev, peer_count)
    local_id = jnp.where(is_live, flat_ids % link_dev, -1)
    capacity = flat_ids.shape[0] // peer_count
    marks = (owner_id[:, None] == jnp.arange(peer_count)[None, :]).astype(jnp.int32)
    slot_id = jnp.sum((jnp.cumsum(marks, axis=0) - marks) * marks, axis=1)
    requests = (
        jnp.full((peer_count, capacity), -1, jnp.int32)
        .at[owner_id, slot_id]
        .set(local_id, mode="drop")
    )
    nothing = jnp.zeros((), jnp.bfloat16)
    every_link = lax.all_gather(own_links, "path", axis=0, tiled=True)
    fetched = jnp.where(is_live[:, None], every_link[jnp.where(is_live, flat_ids, 0)], nothing)
    received = lax.all_to_all(requests, "path", split_axis=0, concat_axis=0, tiled=True)
    projected = jnp.dot(fetched, w_path_in, preferred_element_type=jnp.float32)
    projected = projected.reshape(path_count, hop_count, 3 * width)
    live_grid = is_live.reshape(path_count, hop_count)
    carried = path_state[0].astype(jnp.float32)
    messages = []
    for hop_index in range(hop_count):
        renewed = gated_update(projected[:, hop_index], carried, w_path_hid)
        carried = jnp.where(live_grid[:, hop_index, None], renewed, carried)
        messages.append(carried.astype(jnp.bfloat16))
    path_final = carried.astype(jnp.bfloat16)
    flat_messages = jnp.stack(messages, axis=1).reshape(-1, width)
    outgoing = (
        jnp.zeros((peer_count, capacity, width), jnp.bfloat16)
        .at[owner_id, slot_id]
        .set(flat_messages, mode="drop")
    )
    incoming = lax.all_to_all(outgoing, "path", split_axis=0, concat_axis=0, tiled=True)
    selector = (received.reshape(-1)[None, :] == jnp.arange(link_dev)[:, None]).astype(jnp.bfloat16)
    link_sum = jnp.dot(selector, incoming.reshape(-1, width), preferred_element_type=jnp.float32)
    link_proj = jnp.dot(
        link_sum.astype(jnp.bfloat16), w_link_in, preferred_element_type=jnp.float32
    )
    link_next = gated_update(link_proj, own_links.astype(jnp.float32), w_link_hid).astype(
        jnp.bfloat16
    )
    grad_term = lax.dot_general(
        cotangent[0], path_final, (((0,), (0,)), ((), ())), preferred_element_type=jnp.float32
    )
    grad_whole = lax.psum(grad_term, ("grp", "path"))
    share = grad_whole.shape[0] // peer_count
    read_grad = lax.dynamic_slice_in_dim(grad_whole, lax.axis_index("path") * share, share, 0)
    return (link_next[None], path_final[None], read_grad)


def solution(mesh):
    return jax.shard_map(
        shards,
        mesh=mesh,
        in_specs=(
            P("grp", "path", None),
            P("grp", "path", None),
            P("path", None),
            P(),
            P(),
            P(),
            P(),
            P("grp", "path", None),
        ),
        out_specs=(P("grp", "path", None), P("grp", "path", None), P("path", None)),
        check_vma=False,
    )
```

profile of v0, /device:TPU:1, one launch (start us, length us, event | category | flops | bytes accessed | tf_op | source)
XLA Modules:
  0.0 428.5 jit_solution(9627529892946809395)
XLA Ops:
  7.2 0.0 copy-start
  7.2 0.0 copy-start.1
  7.2 0.0 all-gather.3.cloned.1.call-start
  7.2 0.7 all-gather.3.cloned.1.call-update
  7.9 0.8 copy.20
  8.7 0.1 reshape.190
  8.8 0.1 reshape.189
  8.9 0.1 reshape.188
  9.0 9.0 %reduce-window.6 = s32[32,8,128]{2,1,0:T(8,128)S(1)} reduce-window(s32[32,8,128]{2,1,0:T(8,128)S(1)} %fusion.135, s32[]{:T(128)} %constant.44.clone.1), window={size=1x1x128 pad=0_0x0_0x127_0}, to_apply=%region_0.1 | reduce-window | flops 4161536 | bytes 262148 | tf_op jit(solution)/shard_map/reduce-window
  18.0 0.1 slice.290
  18.1 0.1 copy.23
  18.3 0.1 copy.24
  18.4 0.1 broadcast_add_fusion
  18.6 0.7 multiply_reduce_fusion
  19.4 4.3 %scatter_custom_fusion = s32[1024]{0:T(1024)S(1)} fusion(s32[1024]{0:T(1024)S(1)} %broadcast_select_fusion, s32[1024]{0:T(1024)S(1)} %get-tuple-element.33, s32[]{:T(128)} %constant.26.clone.1), kind=kCustom, calls=%fused_computation.239 | custom fusion | bytes 4100
  23.7 0.7 all_to_all.9
  24.4 13.7 %all-to-all-start = ((s32[32,1,32]{2,1,0:T(1,128)}), s32[32,1,32]{2,1,0:T(1,128)S(1)}, u32[]{:S(2)}, u32[]{:S(2)}) async-start(s32[32,1,32]{2,1,0:T(1,128)} %all_to_all.9), calls=%async_computation | async-start | bytes 32768 | tf_op jit(solution)/shard_map/all_to_all | solution.py:38
  38.1 0.7 broadcast_compare_fusion
  38.9 0.0 copy-done.1
  38.9 1.1 fusion.136
  39.9 80.9 %all-gather.3.cloned.1.call-done = bf16[1,16384,256]{2,1,0:T(8,128)(2,1)} async-done(((bf16[1,512,256]{2,1,0:T(8,128)(2,1)}), bf16[1,16384,256]{2,1,0:T(8,128)(2,1)}) %all-gather.3.cloned.1.call-update) | async-done | bytes 8388624 | tf_op jit(solution)/shard_map/all_gather | solution.py:36
  120.9 7.9 %gather_fusion = bf16[1024,256]{1,0:T(8,128)(2,1)S(1)} fusion(bf16[16384,256]{1,0:T(8,128)(2,1)} %bitcast.116, s32[1024]{0:T(1024)S(1)} %broadcast_clamp_fusion), kind=kCustom, calls=%fused_computation | custom fusion | bytes 1052672 | tf_op jit(solution)/shard_map/gather | solution.py:37
  128.8 0.0 copy-done
  128.8 0.6 convolution_bitcast_fusion
  129.4 0.0 copy-start.5
  129.5 2.1 fusion.170
  131.6 0.0 copy-done.5
  131.7 0.1 bitcast_dynamic-update-slice_fusion.7
  131.8 0.2 fusion.151
  132.0 0.1 bitcast_dynamic-update-slice_fusion.6
  132.2 0.2 fusion.149
  132.4 0.1 bitcast_dynamic-update-slice_fusion.5
  132.5 0.2 fusion.147
  132.8 0.1 bitcast_dynamic-update-slice_fusion.4
  132.9 0.2 fusion.145
  133.2 0.1 bitcast_dynamic-update-slice_fusion.3
  133.3 0.2 fusion.143
  133.5 0.1 bitcast_dynamic-update-slice_fusion.2
  133.6 0.2 fusion.141
  133.9 0.1 bitcast_dynamic-update-slice_fusion.1
  134.0 0.2 fusion.139
  134.2 0.0 copy-start.6
  134.3 0.0 copy-start.2
  134.3 0.0 copy-start.3
  134.3 0.1 bitcast_dynamic-update-slice_fusion
  134.4 0.0 copy-start.4
  134.4 6.4 %scatter_custom_fusion.1 = bf16[1024,256]{1,0:T(8,128)(2,1)} fusion(s32[1024]{0:T(1024)S(1)} %broadcast_select_fusion, bf16[128,8,256]{2,0,1:T(8,128)(2,1)S(1)} %get-tuple-element.9, bf16[]{:T(256)} %constant.50.clone.1), kind=kCustom, calls=%fused_computation.26 | custom fusion | bytes 1048578
  140.8 0.0 all-to-all-done
  140.8 5.3 %all-to-all-start.1 = ((bf16[32,32,256]{2,1,0:T(8,128)(2,1)}), bf16[32,32,256]{2,1,0:T(8,128)(2,1)}, u32[]{:S(2)}, u32[]{:S(2)}) async-start(bf16[32,32,256]{2,1,0:T(8,128)(2,1)} %bitcast.32), calls=%async_computation.1 | async-start | bytes 1048576 | tf_op jit(solution)/shard_map/all_to_all | solution.py:55
  146.2 0.0 all-reduce.2.cloned.1.call-start
  146.2 0.0 copy-done.6
  146.2 0.9 convolution_bitcast_fusion.1
  147.1 0.0 copy-done.4
  147.1 0.0 all-reduce.2.cloned.1.call-update
  147.1 0.4 fusion.23
  147.5 0.5 broadcast.260
  148.0 0.7 reduce.9
  148.7 0.1 eq.44
  148.8 267.0 %all-reduce.2.cloned.1.call-done = f32[128,256]{0,1:T(8,128)} async-done(((f32[128,256]{0,1:T(8,128)}), f32[128,256]{0,1:T(8,128)}) %all-reduce.2.cloned.1.call-update) | async-done | bytes 131088 | tf_op jit(solution)/shard_map/psum | solution.py:67
  415.8 1.0 constant_dynamic-slice_fusion
  416.8 0.7 copy.34
  417.4 0.0 all-to-all-done.1
  417.4 2.2 fusion.2
  419.6 2.0 fusion.27
  (22 shorter events, 0.4 us)
Async XLA Ops:
  7.2 121.6 %copy-start = (bf16[256,768]{1,0:T(8,128)(2,1)S(1)}, bf16[256,768]{1,0:T(8,128)(2,1)}, u32[]{:S(2)}) copy-start(bf16[256,768]{1,0:T(8,128)(2,1)} %param.11) | copy-start | bytes 1179652
  7.2 31.7 %copy-start.1 = (bf16[256,768]{1,0:T(8,128)(2,1)S(1)}, bf16[256,768]{1,0:T(8,128)(2,1)}, u32[]{:S(2)}) copy-start(bf16[256,768]{1,0:T(8,128)(2,1)} %param.12) | copy-start | bytes 1179652
  7.2 113.7 %all-gather.3.cloned.1.call-start = ((), (), s32[]{:S(2)}) async-start(), calls=%async_computation.3 | async-start | bytes 8650752 | tf_op jit(solution)/shard_map/all_gather | solution.py:36
  24.4 116.4 %all-to-all-start = ((s32[32,1,32]{2,1,0:T(1,128)}), s32[32,1,32]{2,1,0:T(1,128)S(1)}, u32[]{:S(2)}, u32[]{:S(2)}) async-start(s32[32,1,32]{2,1,0:T(1,128)} %all_to_all.9), calls=%async_computation | async-start | bytes 32768 | tf_op jit(solution)/shard_map/all_to_all | solution.py:38
  129.4 2.2 copy-start.5
  134.2 12.0 %copy-start.6 = (bf16[1,128,128]{2,1,0:T(8,128)(2,1)S(1)}, bf16[1,128,128]{2,1,0:T(8,128)(2,1)}, u32[]{:S(2)}) copy-start(bf16[1,128,128]{2,1,0:T(8,128)(2,1)} %param.15) | copy-start | bytes 98308
  134.3 12.8 %copy-start.2 = (bf16[1,512,256]{2,1,0:T(8,128)(2,1)S(1)}, bf16[1,512,256]{2,1,0:T(8,128)(2,1)}, u32[]{:S(2)}) copy-start(bf16[1,512,256]{2,1,0:T(8,128)(2,1)} %param.8) | copy-start | bytes 786436
  134.3 12.8 %copy-start.3 = (bf16[256,768]{1,0:T(8,128)(2,1)S(1)}, bf16[256,768]{1,0:T(8,128)(2,1)}, u32[]{:S(2)}) copy-start(bf16[256,768]{1,0:T(8,128)(2,1)} %param.14) | copy-start | bytes 1179652
  134.4 12.6 %copy-start.4 = (bf16[128,256]{1,0:T(8,128)(2,1)}, bf16[128,256]{1,0:T(8,128)(2,1)S(1)}, u32[]{:S(2)}) copy-start(bf16[128,256]{1,0:T(8,128)(2,1)S(1)} %get-tuple-element.10) | copy-start | bytes 196612
  140.8 276.6 %all-to-all-start.1 = ((bf16[32,32,256]{2,1,0:T(8,128)(2,1)}), bf16[32,32,256]{2,1,0:T(8,128)(2,1)}, u32[]{:S(2)}, u32[]{:S(2)}) async-start(bf16[32,32,256]{2,1,0:T(8,128)(2,1)} %bitcast.32), calls=%async_computation.1 | async-start | bytes 1048576 | tf_op jit(solution)/shard_map/all_to_all | solution.py:55
  146.2 269.6 %all-reduce.2.cloned.1.call-start = ((), (), s32[]{:S(2)}) async-start(), calls=%async_computation.2 | async-start | bytes 262144 | tf_op jit(solution)/shard_map/psum | solution.py:67
Sparse Core Ops, SparseCore 0:
  11.2 109.6 all-gather.2
  152.6 263.1 all-reduce.1
where the time goes:
time: 429 us; the launch traced here: 428 us
  waiting for transfers between devices  349 us (81%)
  local copies, waits for them, and re-layouts  25.4 us (6%)
  starting transfers between devices  19.1 us (4%)
  between operations  14.5 us (3%)
  other arithmetic  14.4 us (3%)
  matrix products  6.55 us (2%)
    psum x1, waiting for transfers between devices, shards(): grad_whole = lax.psum(grad_term, ('grp', 'path'))  267 us
    all_gather x1, waiting for transfers between devices, shards(): every_link = lax.all_gather(own_links, 'path', axis=0, tiled=True)  80.9 us
    all_to_all x1, starting transfers between devices, shards(): lax.all_to_all(requests, 'path', split_axis=0, concat_axis=0, tiled=True)  13.7 us
    unnamed x26, local copies, waits for them, and re-layouts  12.4 us
    another operation x3, other arithmetic  9.14 us
  transfers between devices with their start and end apart: 4, of which 2 were waited for; matrix products, arithmetic and copies ran while one was open for 10% of the time, Pallas kernels for 0%

commit v1 on v0

--- a/solution.py
+++ b/solution.py
@@ -33,7 +33,9 @@
         .set(local_id, mode="drop")
     )
     nothing = jnp.zeros((), jnp.bfloat16)
-    every_link = lax.all_gather(own_links, "path", axis=0, tiled=True)
+    every_link = jnp.concatenate(
+        lax.all_to_all(jnp.stack([own_links] * lax.axis_size("path")), "path", 0, 0), axis=0
+    )
     fetched = jnp.where(is_live[:, None], every_link[jnp.where(is_live, flat_ids, 0)], nothing)
     received = lax.all_to_all(requests, "path", split_axis=0, concat_axis=0, tiled=True)
     projected = jnp.dot(fetched, w_path_in, preferred_element_type=jnp.float32)

time: 429 us -> 542 us (1.26)
  waiting for transfers between devices: 349 us -> 440 us
  starting transfers between devices: 19.1 us -> 39.1 us
    all_to_all x0 -> x1, waiting for transfers between devices: none -> 172 us  [shards(): lax.all_to_all(jnp.stack([own_links] * lax.axis_size('path')), 'path', 0, 0)]
    all_gather x1 -> x0, waiting for transfers between devices: 80.9 us -> none  [shards(): every_link = lax.all_gather(own_links, 'path', axis=0, tiled=True)]
    all_to_all x0 -> x1, starting transfers between devices: none -> 14 us  [shards(): lax.all_to_all(jnp.stack([own_links] * lax.axis_size('path')), 'path', 0, 0)]
    unnamed x26 -> x30, local copies, waits for them, and re-layouts: 12.4 us -> 11.8 us
  transfers between devices with their start and end apart: 4 -> 4, of which waited for: 2 -> 2; matrix products, arithmetic and copies ran while one was open for 10% -> 7% of each run, Pallas kernels for 0% -> 0%
where the time goes in v1:
time: 542 us
  waiting for transfers between devices  440 us (81%)
  starting transfers between devices  39.1 us (7%)
  local copies, waits for them, and re-layouts  29.8 us (5%)
  between operations  14.5 us (3%)
  other arithmetic  13 us (2%)
  matrix products  5.71 us (1%)
    psum x1, waiting for transfers between devices, shards(): grad_whole = lax.psum(grad_term, ('grp', 'path'))  268 us
    all_to_all x1, waiting for transfers between devices, shards(): lax.all_to_all(jnp.stack([own_links] * lax.axis_size('path')), 'path', 0, 0)  172 us
    all_to_all x1, starting transfers between devices, shards(): lax.all_to_all(requests, 'path', split_axis=0, concat_axis=0, tiled=True)  15.7 us
    all_to_all x1, starting transfers between devices, shards(): lax.all_to_all(jnp.stack([own_links] * lax.axis_size('path')), 'path', 0, 0)  14 us
    unnamed x30, local copies, waits for them, and re-layouts  11.8 us
  transfers between devices with their start and end apart: 4, of which 2 were waited for; matrix products, arithmetic and copies ran while one was open for 7% of the time, Pallas kernels for 0%

profile of v1, /device:TPU:1, one launch (start us, length us, event | category | flops | bytes accessed | tf_op | source)
XLA Modules:
  0.0 542.0 jit_solution(5224355992175156507)
XLA Ops:
  7.2 0.0 copy-start
  7.2 5.2 stack.30
  12.3 14.0 %all-to-all-start.1 = ((bf16[32,512,256]{2,1,0:T(8,128)(2,1)}), bf16[32,512,256]{2,1,0:T(8,128)(2,1)}, u32[]{:S(2)}, u32[]{:S(2)}) async-start(bf16[32,512,256]{2,1,0:T(8,128)(2,1)} %stack.30), calls=%async_computation.1 | async-start | bytes 16777216 | tf_op jit(solution)/shard_map/all_to_all | solution.py:37
  26.3 0.0 copy-done.7
  26.4 0.1 copy.20
  26.5 0.1 reshape.194
  26.5 0.1 reshape.193
  26.6 0.1 reshape.192
  26.8 9.0 %reduce-window.6 = s32[32,8,128]{2,1,0:T(8,128)S(1)} reduce-window(s32[32,8,128]{2,1,0:T(8,128)S(1)} %fusion.133, s32[]{:T(128)} %constant.44.clone.1), window={size=1x1x128 pad=0_0x0_0x127_0}, to_apply=%region_0.1 | reduce-window | flops 4161536 | bytes 262148 | tf_op jit(solution)/shard_map/reduce-window
  35.8 0.1 slice.290
  35.9 0.1 copy.23
  36.1 0.1 copy.24
  36.2 0.1 broadcast_add_fusion
  36.4 0.0 copy-done.8
  36.4 0.1 multiply_reduce_fusion
  36.5 4.3 scatter_custom_fusion
  40.8 0.7 all_to_all.12
  41.5 0.0 copy-done.1
  41.6 0.0 copy-done.5
  41.6 0.2 fusion.134
  41.8 172.1 %all-to-all-done.1 = bf16[32,512,256]{2,1,0:T(8,128)(2,1)} async-done(((bf16[32,512,256]{2,1,0:T(8,128)(2,1)}), bf16[32,512,256]{2,1,0:T(8,128)(2,1)}, u32[]{:S(2)}, u32[]{:S(2)}) %all-to-all-start.1) | async-done | bytes 8388640 | tf_op jit(solution)/shard_map/all_to_all | solution.py:37
  213.9 15.7 %all-to-all-start = ((s32[32,1,32]{2,1,0:T(1,128)}), s32[32,1,32]{2,1,0:T(1,128)S(1)}, u32[]{:S(2)}, u32[]{:S(2)}) async-start(s32[32,1,32]{2,1,0:T(1,128)} %all_to_all.12), calls=%async_computation | async-start | bytes 32768 | tf_op jit(solution)/shard_map/all_to_all | solution.py:40
  229.6 7.9 %gather_fusion = bf16[1024,256]{1,0:T(8,128)(2,1)S(1)} fusion(bf16[16384,256]{1,0:T(8,128)(2,1)} %bitcast.5, s32[1024]{0:T(1024)S(1)} %broadcast_clamp_fusion), kind=kCustom, calls=%fused_computation | custom fusion | bytes 1052672 | tf_op jit(solution)/shard_map/gather | solution.py:39
  237.5 0.0 copy-done
  237.5 0.6 convolution_bitcast_fusion
  238.2 2.1 fusion.170
  240.3 0.1 bitcast_dynamic-update-slice_fusion.7
  240.5 0.2 fusion.149
  240.7 0.1 bitcast_dynamic-update-slice_fusion.6
  240.8 0.2 fusion.147
  241.1 0.1 bitcast_dynamic-update-slice_fusion.5
  241.2 0.2 fusion.145
  241.5 0.1 bitcast_dynamic-update-slice_fusion.4
  241.6 0.2 fusion.143
  241.8 0.1 bitcast_dynamic-update-slice_fusion.3
  242.0 0.2 fusion.141
  242.2 0.1 bitcast_dynamic-update-slice_fusion.2
  242.3 0.2 fusion.139
  242.6 0.1 bitcast_dynamic-update-slice_fusion.1
  242.7 0.2 fusion.137
  242.9 0.0 copy-start.6
  242.9 0.0 copy-start.2
  243.0 0.0 copy-start.3
  243.0 0.1 bitcast_dynamic-update-slice_fusion
  243.1 0.0 copy-start.4
  243.1 6.4 %scatter_custom_fusion.1 = bf16[1024,256]{1,0:T(8,128)(2,1)} fusion(s32[1024]{0:T(1024)S(1)} %broadcast_select_fusion, bf16[128,8,256]{2,0,1:T(8,128)(2,1)S(1)} %get-tuple-element.9, bf16[]{:T(256)} %constant.50.clone.1), kind=kCustom, calls=%fused_computation.26 | custom fusion | bytes 1048578
  249.5 0.0 all-to-all-done
  249.5 9.3 %all-to-all-start.2 = ((bf16[32,32,256]{2,1,0:T(8,128)(2,1)}), bf16[32,32,256]{2,1,0:T(8,128)(2,1)}, u32[]{:S(2)}, u32[]{:S(2)}) async-start(bf16[32,32,256]{2,1,0:T(8,128)(2,1)} %bitcast.33), calls=%async_computation.2 | async-start | bytes 1048576 | tf_op jit(solution)/shard_map/all_to_all | solution.py:57
  258.9 0.0 all-reduce.2.cloned.1.call-start
  258.9 0.0 copy-done.6
  258.9 0.9 convolution_bitcast_fusion.1
  259.8 0.0 copy-done.4
  259.8 0.0 all-reduce.2.cloned.1.call-update
  259.8 0.0 copy-done.2
  259.8 0.4 fusion.160
  260.2 0.5 broadcast.261
  260.7 0.7 reduce.9
  261.4 0.1 eq.44
  261.5 267.8 %all-reduce.2.cloned.1.call-done = f32[128,256]{0,1:T(8,128)} async-done(((f32[128,256]{0,1:T(8,128)}), f32[128,256]{0,1:T(8,128)}) %all-reduce.2.cloned.1.call-update) | async-done | bytes 131088 | tf_op jit(solution)/shard_map/psum | solution.py:69
  529.3 1.0 constant_dynamic-slice_fusion
  530.3 0.7 copy.34
  531.0 0.0 all-to-all-done.2
  531.0 2.2 fusion.2
  533.1 2.0 fusion.25
  (26 shorter events, 0.4 us)
Async XLA Ops:
  7.2 230.3 %copy-start = (bf16[256,768]{1,0:T(8,128)(2,1)S(1)}, bf16[256,768]{1,0:T(8,128)(2,1)}, u32[]{:S(2)}) copy-start(bf16[256,768]{1,0:T(8,128)(2,1)} %param.11) | copy-start | bytes 1179652
  12.3 14.0 %copy-start.7 = (s32[128,8]{0,1:T(8,128)S(1)}, s32[128,8]{0,1:T(8,128)}, u32[]{:S(2)}) copy-start(s32[128,8]{0,1:T(8,128)} %param.10) | copy-start | bytes 12292
  12.3 24.0 %copy-start.8 = (s32[2]{0:T(128)S(1)}, s32[2]{0:T(128)}, u32[]{:S(2)}) copy-start(s32[2]{0:T(128)} %constant.58) | copy-start | bytes 28
  12.3 29.2 %copy-start.1 = (bf16[256,768]{1,0:T(8,128)(2,1)S(1)}, bf16[256,768]{1,0:T(8,128)(2,1)}, u32[]{:S(2)}) copy-start(bf16[256,768]{1,0:T(8,128)(2,1)} %param.12) | copy-start | bytes 1179652
  12.3 29.2 %copy-start.5 = (bf16[1,128,256]{2,1,0:T(8,128)(2,1)S(1)}, bf16[1,128,256]{2,1,0:T(8,128)(2,1)}, u32[]{:S(2)}) copy-start(bf16[1,128,256]{2,1,0:T(8,128)(2,1)} %param.9) | copy-start | bytes 196612
  12.3 201.5 %all-to-all-start.1 = ((bf16[32,512,256]{2,1,0:T(8,128)(2,1)}), bf16[32,512,256]{2,1,0:T(8,128)(2,1)}, u32[]{:S(2)}, u32[]{:S(2)}) async-start(bf16[32,512,256]{2,1,0:T(8,128)(2,1)} %stack.30), calls=%async_computation.1 | async-start | bytes 16777216 | tf_op jit(solution)/shard_map/all_to_all | solution.py:37
  213.9 35.7 %all-to-all-start = ((s32[32,1,32]{2,1,0:T(1,128)}), s32[32,1,32]{2,1,0:T(1,128)S(1)}, u32[]{:S(2)}, u32[]{:S(2)}) async-start(s32[32,1,32]{2,1,0:T(1,128)} %all_to_all.12), calls=%async_computation | async-start | bytes 32768 | tf_op jit(solution)/shard_map/all_to_all | solution.py:40
  242.9 16.0 %copy-start.6 = (bf16[1,128,128]{2,1,0:T(8,128)(2,1)S(1)}, bf16[1,128,128]{2,1,0:T(8,128)(2,1)}, u32[]{:S(2)}) copy-start(bf16[1,128,128]{2,1,0:T(8,128)(2,1)} %param.15) | copy-start | bytes 98308
  242.9 16.9 %copy-start.2 = (bf16[1,512,256]{2,1,0:T(8,128)(2,1)S(1)}, bf16[1,512,256]{2,1,0:T(8,128)(2,1)}, u32[]{:S(2)}) copy-start(bf16[1,512,256]{2,1,0:T(8,128)(2,1)} %param.8) | copy-start | bytes 786436
  243.0 16.9 %copy-start.3 = (bf16[256,768]{1,0:T(8,128)(2,1)S(1)}, bf16[256,768]{1,0:T(8,128)(2,1)}, u32[]{:S(2)}) copy-start(bf16[256,768]{1,0:T(8,128)(2,1)} %param.14) | copy-start | bytes 1179652
  243.1 16.7 %copy-start.4 = (bf16[128,256]{1,0:T(8,128)(2,1)}, bf16[128,256]{1,0:T(8,128)(2,1)S(1)}, u32[]{:S(2)}) copy-start(bf16[128,256]{1,0:T(8,128)(2,1)S(1)} %get-tuple-element.10) | copy-start | bytes 196612
  249.5 281.4 %all-to-all-start.2 = ((bf16[32,32,256]{2,1,0:T(8,128)(2,1)}), bf16[32,32,256]{2,1,0:T(8,128)(2,1)}, u32[]{:S(2)}, u32[]{:S(2)}) async-start(bf16[32,32,256]{2,1,0:T(8,128)(2,1)} %bitcast.33), calls=%async_computation.2 | async-start | bytes 1048576 | tf_op jit(solution)/shard_map/all_to_all | solution.py:57
  258.9 270.4 %all-reduce.2.cloned.1.call-start = ((), (), s32[]{:S(2)}) async-start(), calls=%async_computation.3 | async-start | bytes 262144 | tf_op jit(solution)/shard_map/psum | solution.py:69
Sparse Core Ops, SparseCore 0:
  265.3 263.9 all-reduce.1
